TPU v7x, 256 devices: a whole 4x4x8 slice. The times are simulated.
256 devices in a mesh: seq: 32 (over z_hi, x, core), uly: 8 (over y, z_lo).
Axes of the slice: x: 4, y: 4, z: 8 (z_hi: 4, z_lo: 2; z = z_hi * 2 + z_lo), core: 2. Of those that a mesh axis runs over, the one named last changes fastest.
Arguments:
- normed: bfloat16 [32768, 5376], P('seq', 'uly'), may hold values from -6 to 6
- q_raw: bfloat16 [32768, 2048], P('seq', 'uly'), may hold values from -6 to 6
- key_weight: bfloat16 [5376, 1024], P('uly', 'seq'), may hold values from -0.078125 to 0.078125
- value_weight: bfloat16 [5376, 1024], P('uly', 'seq'), may hold values from -0.078125 to 0.078125
- q_gain: float32 [128], replicated, may hold values from 0.1 to 1.9
- k_gain: float32 [128], replicated, may hold values from 0.1 to 1.9
- segment_ids: int32 [32768], replicated, may hold values from 0 to 1, as said below
- grad_out: bfloat16 [32768, 2048], P('seq', 'uly'), may hold values from -6 to 6
Outputs:
- attention: bfloat16 [32768, 2048], P('seq', 'uly')
- grad_normed: bfloat16 [32768, 5376], P('seq', 'uly')
- grad_q: bfloat16 [32768, 2048], P('seq', 'uly')
- grad_key_weight: float32 [5376, 1024], P('uly', 'seq')
- grad_value_weight: float32 [5376, 1024], P('uly', 'seq')
Inputs may be any that keep to these rules, and one draw needn't show every extreme that they name: `segment_ids`: 0 up to one position and 1 from it on; that position lies between 8192 and 24576.
All inputs are finite; a program needn't handle non-finite values.
Results may differ from a plain program's by a relative error of at most 0.025.
Values may be sent and summed in bfloat16 or wider, within the bound.
A program may use at most 128 MiB of HBM per device.

v0:
```python
import jax
import jax.numpy as jnp
from jax import lax
from jax.sharding import PartitionSpec as P

HD = 128
WINDOW = 1024
epsilon = 1e-06
query_scale = 168.0 ** (-0.5)


def from_behind(array, axis, by):
    devices = lax.axis_size(axis)
    pairs = [(i, i + by) for i in range(devices) if 0 <= i + by < devices]
    return lax.ppermute(array, axis, pairs)


def normalize(raw_vals, gain, factor):
    mean_sq = jnp.mean(raw_vals * raw_vals, axis=-1, keepdims=True)
    return raw_vals * lax.rsqrt(mean_sq + epsilon) * gain * factor


def attend_block(
    queries, key_block, value_block, grad_block, query_pos, key_pos, query_seg, key_seg
):
    scores = jnp.einsum("bhge,lhe->hgbl", queries, key_block, preferred_element_type=jnp.float32)
    allowed = (
        (key_pos[None, :] <= query_pos[:, None])
        & (key_pos[None, :] > query_pos[:, None] - WINDOW)
        & (key_seg[None, :] == query_seg[:, None])
    )
    exp_scores = jnp.where(allowed[None, None], jnp.exp(scores), 0.0)
    probs = exp_scores / jnp.sum(exp_scores, axis=-1, keepdims=True)
    weights = probs.astype(jnp.bfloat16)
    attended = jnp.einsum(
        "hgbl,lhe->bhge", weights, value_block, preferred_element_type=jnp.float32
    ).astype(jnp.bfloat16)
    dprob = jnp.einsum(
        "bhge,lhe->hgbl", grad_block, value_block, preferred_element_type=jnp.float32
    )
    delta_row = jnp.sum(probs * dprob, axis=-1, keepdims=True)
    dscore = (probs * (dprob - delta_row)).astype(jnp.bfloat16)
    dquery = jnp.einsum("hgbl,lhe->bhge", dscore, key_block, preferred_element_type=jnp.float32)
    dkey = jnp.einsum("hgbl,bhge->lhe", dscore, queries, preferred_element_type=jnp.float32)
    dvalue = jnp.einsum("hgbl,bhge->lhe", weights, grad_block, preferred_element_type=jnp.float32)
    return (attended, dquery, dkey, dvalue)


def body(normed, q_raw, key_weight, value_weight, q_gain, k_gain, segment_ids, grad_out):
    rows_here = normed.shape[0]
    heads_here = q_raw.shape[1] // (2 * HD)
    seq_index = lax.axis_index("seq")
    base_row = seq_index * rows_here
    weight_pair = (
        lax.all_gather(key_weight, "seq", axis=1, tiled=True),
        lax.all_gather(value_weight, "seq", axis=1, tiled=True),
    )
    key_term = jnp.dot(normed, weight_pair[0], preferred_element_type=jnp.float32)
    value_term = jnp.dot(normed, weight_pair[1], preferred_element_type=jnp.float32)
    key_raw, value_raw = (
        lax.psum_scatter(
            key_term.astype(jnp.bfloat16), "uly", scatter_dimension=1, tiled=True
        ).astype(jnp.float32),
        lax.psum_scatter(
            value_term.astype(jnp.bfloat16), "uly", scatter_dimension=1, tiled=True
        ).astype(jnp.float32),
    )
    key_in = key_raw.reshape(rows_here, heads_here, HD)
    keys_bf = normalize(key_in, k_gain, 1.0).astype(jnp.bfloat16)
    values_bf = value_raw.reshape(rows_here, heads_here, HD).astype(jnp.bfloat16)
    query_in = q_raw.astype(jnp.float32).reshape(rows_here, heads_here, 2, HD)
    queries = normalize(query_in, q_gain, query_scale).astype(jnp.bfloat16)
    grad_heads = grad_out.reshape(rows_here, heads_here, 2, HD)
    stacked = jnp.stack([keys_bf, values_bf])
    pieces = []
    distance = 1
    pieces.append(from_behind(stacked, "seq", distance))
    pieces.append(stacked)
    extended = jnp.concatenate(pieces, axis=1)
    block_rows = min(512, rows_here)
    span_rows = block_rows + WINDOW
    count_blocks = rows_here // block_rows
    seg_pad = jnp.concatenate([jnp.full((WINDOW,), -1, jnp.int32), segment_ids])
    query_seg_all = lax.dynamic_slice_in_dim(segment_ids, base_row, rows_here, 0)
    key_seg_all = lax.dynamic_slice_in_dim(seg_pad, base_row, WINDOW + rows_here, 0)

    def step(grad_acc, block_index):
        begin_row = block_index * block_rows
        query_pos = base_row + begin_row + jnp.arange(block_rows, dtype=jnp.int32)
        key_pos = base_row + begin_row - WINDOW + jnp.arange(span_rows, dtype=jnp.int32)
        key_block = lax.dynamic_slice_in_dim(extended, begin_row, span_rows, 1)
        attended, dquery, dkey, dvalue = attend_block(
            lax.dynamic_slice_in_dim(queries, begin_row, block_rows, 0),
            key_block[0],
            key_block[1],
            lax.dynamic_slice_in_dim(grad_heads, begin_row, block_rows, 0),
            query_pos,
            key_pos,
            lax.dynamic_slice_in_dim(query_seg_all, begin_row, block_rows, 0),
            lax.dynamic_slice_in_dim(key_seg_all, begin_row, span_rows, 0),
        )
        update = jnp.stack([dkey, dvalue])
        grad_acc = lax.dynamic_update_slice_in_dim(
            grad_acc,
            lax.dynamic_slice_in_dim(grad_acc, begin_row, span_rows, 1) + update,
            begin_row,
            1,
        )
        return (grad_acc, (attended, dquery))

    zero_acc = jnp.zeros((2, WINDOW + rows_here, heads_here, HD), jnp.float32)
    grad_acc, (attended, dquery) = lax.scan(
        step, zero_acc, jnp.arange(count_blocks, dtype=jnp.int32)
    )
    attention = attended.reshape(rows_here, 2 * heads_here * HD)
    dquery = dquery.reshape(rows_here, heads_here, 2, HD)
    own_grads = grad_acc[:, WINDOW:]
    offset_row = 0
    distance = 1
    first_row = max(0, distance * rows_here - WINDOW)
    piece_rows = rows_here - first_row
    outgoing = grad_acc[:, offset_row : offset_row + piece_rows]
    returned = from_behind(outgoing.astype(jnp.bfloat16), "seq", -distance).astype(outgoing.dtype)
    own_grads = own_grads.at[:, first_row:].add(returned)
    _, pull_query = jax.vjp(lambda raw_vals: normalize(raw_vals, q_gain, query_scale), query_in)
    grad_q = pull_query(dquery)[0].astype(jnp.bfloat16).reshape(rows_here, 2 * heads_here * HD)
    _, pull_key = jax.vjp(lambda raw_vals: normalize(raw_vals, k_gain, 1.0), key_in)
    key_grad = pull_key(own_grads[0])[0].astype(jnp.bfloat16).reshape(rows_here, heads_here * HD)
    value_grad = own_grads[1].astype(jnp.bfloat16).reshape(rows_here, heads_here * HD)
    key_all, value_all = (
        lax.all_gather(key_grad, "uly", axis=1, tiled=True),
        lax.all_gather(value_grad, "uly", axis=1, tiled=True),
    )
    dims_last = (((1,), (1,)), ((), ()))
    total = lax.dot_general(key_all, weight_pair[0], dims_last, preferred_element_type=jnp.float32)
    total = total + lax.dot_general(
        value_all, weight_pair[1], dims_last, preferred_element_type=jnp.float32
    )
    grad_normed = total.astype(jnp.bfloat16)
    dims_first = (((0,), (0,)), ((), ()))
    key_part = lax.dot_general(normed, key_all, dims_first, preferred_element_type=jnp.float32)
    value_part = lax.dot_general(normed, value_all, dims_first, preferred_element_type=jnp.float32)
    grad_key_weight = lax.psum_scatter(
        key_part.astype(jnp.bfloat16), "seq", scatter_dimension=1, tiled=True
    ).astype(jnp.float32)
    grad_value_weight = lax.psum_scatter(
        value_part.astype(jnp.bfloat16), "seq", scatter_dimension=1, tiled=True
    ).astype(jnp.float32)
    return (attention, grad_normed, grad_q, grad_key_weight, grad_value_weight)


def solution(mesh):
    return jax.shard_map(
        body,
        mesh=mesh,
        in_specs=(
            P("seq", "uly"),
            P("seq", "uly"),
            P("uly", "seq"),
            P("uly", "seq"),
            P(),
            P(),
            P(),
            P("seq", "uly"),
        ),
        out_specs=(
            P("seq", "uly"),
            P("seq", "uly"),
            P("seq", "uly"),
            P("uly", "seq"),
            P("uly", "seq"),
        ),
        check_vma=False,
    )
```

profile of v0, /device:TPU:8, one launch (start us, length us, event | category | flops | bytes accessed | tf_op | source)
XLA Modules:
  0.0 660.0 jit_solution(17294904801628966147)
XLA Ops:
  8.7 57.9 %all-gather.6.cloned.1.call-done = bf16[672,1024]{0,1:T(8,128)(2,1)} async-done(((bf16[672,32]{0,1:T(8,128)(2,1)}), bf16[672,1024]{0,1:T(8,128)(2,1)}) %all-gather.6.cloned.1.call-update) | async-done | bytes 1376272 | tf_op jit(solution)/shard_map/all_gather | solution.py:55
  66.6 3.3 convolution_convert_fusion.1
  69.9 2.6 copy.101
  72.5 46.9 %all-gather.8.cloned.1.call-done = bf16[672,1024]{0,1:T(8,128)(2,1)} async-done(((bf16[672,32]{0,1:T(8,128)(2,1)}), bf16[672,1024]{0,1:T(8,128)(2,1)}) %all-gather.8.cloned.1.call-update) | async-done | bytes 1376272 | tf_op jit(solution)/shard_map/all_gather | solution.py:56
  119.5 3.3 convolution_convert_fusion
  122.7 2.6 copy.103
  126.8 45.8 %reduce-scatter.13.cloned.1.call-done = bf16[128,1024]{1,0:T(8,128)(2,1)} async-done(((bf16[1024,1024]{1,0:T(8,128)(2,1)}), bf16[128,1024]{1,0:T(8,128)(2,1)}) %reduce-scatter.13.cloned.1.call-update) | async-done | bytes 262160
  174.0 55.4 %reduce-scatter.15.cloned.1.call-done = bf16[128,1024]{1,0:T(8,128)(2,1)} async-done(((bf16[1024,1024]{1,0:T(8,128)(2,1)}), bf16[128,1024]{1,0:T(8,128)(2,1)}) %reduce-scatter.15.cloned.1.call-update) | async-done | bytes 262160
  229.4 1.8 copy.104
  231.4 1.8 pad_maximum_fusion
  233.2 2.6 collective-permute-start
  236.5 2.0 copy.79
  239.6 2.2 maximum_maximum_fusion
  243.2 79.3 %while.19 = (s32[]{:T(128)}, f32[2,2048,1,128]{3,1,2,0:T(8,128)}, bf16[2,512,1,2,128]{4,3,1,0,2:T(2,128)(2,1)}, f32[2,512,1,2,128]{1,4,3,2,0:T(8,128)}, s32[2]{0...) while((s32[]{:T(128)}, f32[2,2048,1,128]{3,1,2,0:T(8,128)}, ...), condition=%wide.region_7.8_spmd, body=%wide.region_4.7_spmd.sunk | while | flops 2447507968 | bytes 149759104 | solution.py:112
  245.5 5.4 fusion.90
  251.0 5.3 fusion.92
  256.3 2.0 fusion.93
  258.3 3.2 convolution_bitcast_fusion.3
  261.6 2.7 fusion.91
  265.5 1.9 copy.127
  267.4 2.7 maximum_add_fusion.2
  270.1 1.9 copy.128
  274.4 2.5 fusion.95
  276.9 4.7 fusion.94
  285.2 5.4 fusion.90
  290.7 5.3 fusion.92
  296.0 2.0 fusion.93
  298.0 3.2 convolution_bitcast_fusion.3
  301.2 2.7 fusion.91
  305.2 1.9 copy.127
  307.0 2.7 maximum_add_fusion.2
  309.8 1.9 copy.128
  314.1 2.5 fusion.95
  316.6 4.7 fusion.94
  323.9 1.5 collective-permute-start.1
  325.4 5.3 collective-permute-done.1
  334.2 74.7 %all-gather.10.cloned.1.call-done = bf16[1024,1024]{1,0:T(8,128)(2,1)} async-done(((bf16[1024,128]{1,0:T(8,128)(2,1)}), bf16[1024,1024]{1,0:T(8,128)(2,1)}) %all-gather.10.cloned.1.call-update) | async-done | bytes 2097168 | tf_op jit(solution)/shard_map/all_gather | solution.py:131
  408.9 3.2 fusion.46
  412.1 1.6 copy.105
  413.7 51.5 %all-gather.12.cloned.1.call-done = bf16[1,1024,1,1024]{3,1,2,0:T(8,128)(2,1)} async-done(((bf16[1,1024,1,128]{3,1,2,0:T(8,128)(2,1)}), bf16[1,1024,1,1024]{3,1,2,0:T(8,128)(2,1)}) %all-gather.12.cloned.1.call-update) | async-done | bytes 2097168 | tf_op jit(solution)/shard_map/all_gather | solution.py:132
  465.2 4.3 fusion.47
  469.5 2.6 copy.107
  473.5 1.8 copy.85
  475.2 1.6 copy.87
  480.8 3.9 fusion.41
  484.7 2.7 add_convert_fusion
  487.5 72.3 %reduce-scatter.17.cloned.1.call-done = bf16[32,672]{1,0:T(8,128)(2,1)} async-done(((bf16[1024,672]{1,0:T(8,128)(2,1)}), bf16[32,672]{1,0:T(8,128)(2,1)}) %reduce-scatter.17.cloned.1.call-update) | async-done | bytes 43024
  561.5 89.9 %reduce-scatter.19.cloned.1.call-done = bf16[32,672]{1,0:T(8,128)(2,1)} async-done(((bf16[1024,672]{1,0:T(8,128)(2,1)}), bf16[32,672]{1,0:T(8,128)(2,1)}) %reduce-scatter.19.cloned.1.call-update) | async-done | bytes 43024
  (166 shorter events, 34.6 us)
Async XLA Ops:
  7.2 59.4 %copy-start = (bf16[1024,672]{0,1:T(8,128)(2,1)S(1)}, bf16[1024,672]{0,1:T(8,128)(2,1)}, u32[]{:S(2)}) copy-start(bf16[1024,672]{0,1:T(8,128)(2,1)} %param.14) | copy-start | bytes 4128772
  7.2 59.4 %all-gather.6.cloned.1.call-start = ((), (), s32[]{:S(2)}) async-start(), calls=%async_computation.4 | async-start | bytes 1622016 | tf_op jit(solution)/shard_map/all_gather | solution.py:55
  7.9 111.6 %all-gather.8.cloned.1.call-start = ((), (), s32[]{:S(2)}) async-start(), calls=%async_computation.5 | async-start | bytes 1622016 | tf_op jit(solution)/shard_map/all_gather | solution.py:56
  8.7 163.9 %reduce-scatter.13.cloned.1.call-start = ((), (), s32[]{:S(2)}) async-start(), calls=%async_computation.8 | async-start | bytes 2359296
  72.5 156.9 %reduce-scatter.15.cloned.1.call-start = ((), (), s32[]{:S(2)}) async-start(), calls=%async_computation.9 | async-start | bytes 2359296
  125.3 283.5 %all-gather.10.cloned.1.call-start = ((), (), s32[]{:S(2)}) async-start(), calls=%async_computation.6 | async-start | bytes 2359296 | tf_op jit(solution)/shard_map/all_gather | solution.py:131
  126.6 112.0 %copy-start.9 = (bf16[1024,256]{0,1:T(8,128)(2,1)}, bf16[1024,256]{0,1:T(8,128)(2,1)S(1)}, u32[]{:S(2)}) copy-start(bf16[1024,256]{0,1:T(8,128)(2,1)S(1)} %copy.78) | copy-start | bytes 1572868
  126.6 104.6 %copy-start.27 = (f32[128]{0:T(128)S(1)}, f32[128]{0:T(128)}, u32[]{:S(2)}) copy-start(f32[128]{0:T(128)} %param.19) | copy-start | bytes 1540
  126.7 111.8 %copy-start.7 = (f32[1024,256]{0,1:T(8,128)}, f32[1024,256]{0,1:T(8,128)S(1)}, u32[]{:S(2)}) copy-start(f32[1024,256]{0,1:T(8,128)S(1)} %convert_element_type.99) | copy-start | bytes 3145732
  126.8 111.7 %copy-start.21 = (f32[1024,2]{0,1:T(2,128)}, f32[1024,2]{0,1:T(2,128)S(1)}, u32[]{:S(2)}) copy-start(f32[1024,2]{0,1:T(2,128)S(1)} %multiply_reduce_fusion.1) | copy-start | bytes 24580
  126.8 111.7 %copy-start.29 = (f32[128]{0:T(128)S(1)}, f32[128]{0:T(128)}, u32[]{:S(2)}) copy-start(f32[128]{0:T(128)} %param.18) | copy-start | bytes 1540
  173.7 65.8 %copy-start.11 = (bf16[1024,128]{1,0:T(8,128)(2,1)}, bf16[1024,128]{1,0:T(8,128)(2,1)S(1)}, u32[]{:S(2)}) copy-start(bf16[1024,128]{1,0:T(8,128)(2,1)S(1)} %copy.102) | copy-start | bytes 786436
  174.0 59.2 %copy-start.25 = (f32[1024]{0:T(1024)}, f32[1024]{0:T(1024)S(1)}, u32[]{:S(2)}) copy-start(f32[1024]{0:T(1024)S(1)} %fusion.52) | copy-start | bytes 12292
  174.0 59.2 %copy-start.23 = (f32[1024]{0:T(1024)}, f32[1024]{0:T(1024)S(1)}, u32[]{:S(2)}) copy-start(f32[1024]{0:T(1024)S(1)} %fusion.59) | copy-start | bytes 12292
  233.2 6.4 collective-permute-start
  239.5 3.6 dynamic-slice-start
  245.5 5.4 copy-start.3
  251.0 5.3 slice-start
  251.0 5.3 slice-start.1
  251.0 5.3 copy-start.4
  258.3 3.3 copy-start.1
  258.3 3.3 copy-start.15
  261.6 2.7 copy-start.6
  271.9 2.5 copy-start.2
  274.4 2.5 copy-start.5
  276.9 4.9 copy-start.16
  285.2 5.4 copy-start.3
  290.6 5.3 slice-start
  290.6 5.3 slice-start.1
  290.7 5.3 copy-start.4
  298.0 3.3 copy-start.1
  298.0 3.3 copy-start.15
  301.2 2.7 copy-start.6
  314.1 2.5 copy-start.5
  316.6 4.9 copy-start.16
  322.5 9.5 %copy-start.12 = (bf16[1024,128]{1,0:T(8,128)(2,1)S(1)}, bf16[1024,128]{1,0:T(8,128)(2,1)}, u32[]{:S(2)}) copy-start(bf16[1024,128]{1,0:T(8,128)(2,1)} %copy-done.11) | copy-start | bytes 786436
  322.5 9.5 %copy-start.28 = (f32[128]{0:T(128)S(1)}, f32[128]{0:T(128)}, u32[]{:S(2)}) copy-start(f32[128]{0:T(128)} %param.19) | copy-start | bytes 1540
  322.5 9.7 %copy-start.26 = (f32[1024]{0:T(1024)S(1)}, f32[1024]{0:T(1024)}, u32[]{:S(2)}) copy-start(f32[1024]{0:T(1024)} %copy-done.25) | copy-start | bytes 12292
  322.5 9.8 %copy-start.24 = (f32[1024]{0:T(1024)S(1)}, f32[1024]{0:T(1024)}, u32[]{:S(2)}) copy-start(f32[1024]{0:T(1024)} %copy-done.23) | copy-start | bytes 12292
  323.9 6.8 %collective-permute-start.1 = (bf16[2,1024,1,128]{3,1,2,0:T(8,128)(2,1)S(1)}, bf16[2,1024,1,128]{3,1,2,0:T(8,128)(2,1)S(1)}, u32[]{:S(2)}, u32[]{:S(2)}) collective-permute-start(bf16[2,1024,1,128]{3,1,2,0:T(8,128)(2,1)S(1)} %slice.69), channel_id=1, source_target_pairs={{8,0},{16,8},{24,16},{32,24},{40,32},{48,40},{56,48},{64,56},{72,6... | collective-permute-start | bytes 1572872 | tf_op jit(solution)/shard_map/ppermute | solution.py:15
  333.4 131.8 %all-gather.12.cloned.1.call-start = ((), (), s32[]{:S(2)}) async-start(), calls=%async_computation.7 | async-start | bytes 2359296 | tf_op jit(solution)/shard_map/all_gather | solution.py:132
  334.2 225.7 %reduce-scatter.17.cloned.1.call-start = ((), (), s32[]{:S(2)}) async-start(), calls=%async_computation.10 | async-start | bytes 1622016
  413.7 237.8 %reduce-scatter.19.cloned.1.call-start = ((), (), s32[]{:S(2)}) async-start(), calls=%async_computation.11 | async-start | bytes 1622016
  469.4 2.7 copy-start.30
  469.5 2.7 copy-start.13
  475.2 3.2 copy-start.8
  480.8 3.9 copy-start.31
  480.8 3.9 copy-start.32
  (9 other events, 12.7 us)
Sparse Core Ops, SparseCore 0:
  10.6 55.9 all-gather.5
  69.1 50.2 all-gather.7
  122.0 50.5 reduce-scatter.12
  175.0 54.3 reduce-scatter.14
  333.5 75.3 all-gather.9
  411.0 54.1 all-gather.11
  469.0 90.7 reduce-scatter.16
  563.6 87.7 reduce-scatter.18
where the time goes:
time: 661 us; the launch traced here: 660 us
  waiting for transfers between devices  501 us (76%)
  matrix products  68.2 us (10%)
  local copies, waits for them, and re-layouts  50 us (8%)
  other arithmetic  20.2 us (3%)
  between operations  14.5 us (2%)
    unnamed x12, waiting for transfers between devices  265 us
    all_gather x1, waiting for transfers between devices, body(): lax.all_gather(key_grad, 'uly', axis=1, tiled=True)  74.7 us
    all_gather x1, waiting for transfers between devices, body(): lax.all_gather(key_weight, 'seq', axis=1, tiled=True)  57.9 us
    all_gather x1, waiting for transfers between devices, body(): lax.all_gather(value_grad, 'uly', axis=1, tiled=True)  51.5 us
    all_gather x1, waiting for transfers between devices, body(): lax.all_gather(value_weight, 'seq', axis=1, tiled=True)  46.9 us
    unnamed x63, local copies, waits for them, and re-layouts  22.4 us
  transfers between devices with their start and end apart: 10, of which 9 were waited for; matrix products, arithmetic and copies ran while one was open for 7% of the time, Pallas kernels for 0%

commit v1 on v0

--- a/solution.py
+++ b/solution.py
@@ -128,7 +128,9 @@
     key_grad = pull_key(own_grads[0])[0].astype(jnp.bfloat16).reshape(rows_here, heads_here * HD)
     value_grad = own_grads[1].astype(jnp.bfloat16).reshape(rows_here, heads_here * HD)
     key_all, value_all = (
-        lax.all_gather(key_grad, "uly", axis=1, tiled=True),
+        jnp.concatenate(
+            lax.all_to_all(jnp.stack([key_grad] * lax.axis_size("uly")), "uly", 0, 0), axis=1
+        ),
         lax.all_gather(value_grad, "uly", axis=1, tiled=True),
     )
     dims_last = (((1,), (1,)), ((), ()))

time: 661 us -> 614 us (0.929)
  waiting for transfers between devices: 501 us -> 445 us
    all_gather x1 -> x0, waiting for transfers between devices: 74.7 us -> none  [body(): lax.all_gather(key_grad, 'uly', axis=1, tiled=True)]
    all_to_all x0 -> x1, waiting for transfers between devices: none -> 19.7 us  [body(): lax.all_to_all(jnp.stack([key_grad] * lax.axis_size('uly')), 'uly', 0, 0)]
    unnamed x12 -> x11, waiting for transfers between devices: 265 us -> 263 us
    unnamed x63 -> x61, local copies, waits for them, and re-layouts: 22.4 us -> 22.4 us
  transfers between devices with their start and end apart: 10 -> 10, of which waited for: 9 -> 9; matrix products, arithmetic and copies ran while one was open for 7% -> 8% of each run, Pallas kernels for 0% -> 0%
where the time goes in v1:
time: 614 us; the launch traced here: 613 us
  waiting for transfers between devices  445 us (72%)
  matrix products  69.8 us (11%)
  local copies, waits for them, and re-layouts  51.9 us (8%)
  other arithmetic  19.5 us (3%)
  between operations  14.5 us (2%)
  starting transfers between devices  10.8 us (2%)
    unnamed x11, waiting for transfers between devices  263 us
    all_gather x1, waiting for transfers between devices, body(): lax.all_gather(key_weight, 'seq', axis=1, tiled=True)  57.9 us
    all_gather x1, waiting for transfers between devices, body(): lax.all_gather(value_grad, 'uly', axis=1, tiled=True)  52.2 us
    all_gather x1, waiting for transfers between devices, body(): lax.all_gather(value_weight, 'seq', axis=1, tiled=True)  46.9 us
    unnamed x61, local copies, waits for them, and re-layouts  22.4 us
    all_to_all x1, waiting for transfers between devices, body(): lax.all_to_all(jnp.stack([key_grad] * lax.axis_size('uly')), 'uly', 0, 0)  19.7 us
  transfers between devices with their start and end apart: 10, of which 9 were waited for; matrix products, arithmetic and copies ran while one was open for 8% of the time, Pallas kernels for 0%

profile of v1, /device:TPU:8, one launch (start us, length us, event | category | flops | bytes accessed | tf_op | source)
XLA Modules:
  0.0 613.2 jit_solution(3578456708252960661)
XLA Ops:
  8.7 57.9 %all-gather.5.cloned.1.call-done = bf16[672,1024]{0,1:T(8,128)(2,1)} async-done(((bf16[672,32]{0,1:T(8,128)(2,1)}), bf16[672,1024]{0,1:T(8,128)(2,1)}) %all-gather.5.cloned.1.call-update) | async-done | bytes 1376272 | tf_op jit(solution)/shard_map/all_gather | solution.py:55
  66.6 3.3 convolution_convert_fusion.1
  69.9 2.6 copy.104
  72.5 46.9 %all-gather.7.cloned.1.call-done = bf16[672,1024]{0,1:T(8,128)(2,1)} async-done(((bf16[672,32]{0,1:T(8,128)(2,1)}), bf16[672,1024]{0,1:T(8,128)(2,1)}) %all-gather.7.cloned.1.call-update) | async-done | bytes 1376272 | tf_op jit(solution)/shard_map/all_gather | solution.py:56
  119.5 3.3 convolution_convert_fusion
  122.7 2.6 copy.106
  126.8 45.8 %reduce-scatter.13.cloned.1.call-done = bf16[128,1024]{1,0:T(8,128)(2,1)} async-done(((bf16[1024,1024]{1,0:T(8,128)(2,1)}), bf16[128,1024]{1,0:T(8,128)(2,1)}) %reduce-scatter.13.cloned.1.call-update) | async-done | bytes 262160
  174.0 55.4 %reduce-scatter.15.cloned.1.call-done = bf16[128,1024]{1,0:T(8,128)(2,1)} async-done(((bf16[1024,1024]{1,0:T(8,128)(2,1)}), bf16[128,1024]{1,0:T(8,128)(2,1)}) %reduce-scatter.15.cloned.1.call-update) | async-done | bytes 262160
  229.4 1.8 copy.107
  231.4 1.8 pad_maximum_fusion
  233.2 2.6 collective-permute-start
  236.5 2.0 copy.81
  239.6 2.2 maximum_maximum_fusion
  243.2 79.5 %while.19 = (s32[]{:T(128)}, f32[2,2048,1,128]{3,1,2,0:T(8,128)}, bf16[2,512,1,2,128]{4,3,1,0,2:T(2,128)(2,1)}, f32[2,512,1,2,128]{1,4,3,2,0:T(8,128)}, s32[2]{0...) while((s32[]{:T(128)}, f32[2,2048,1,128]{3,1,2,0:T(8,128)}, ...), condition=%wide.region_7.8_spmd, body=%wide.region_4.7_spmd.sunk | while | flops 2447507968 | bytes 149759104 | solution.py:112
  245.6 5.4 fusion.90
  251.1 5.2 fusion.92
  256.4 2.0 fusion.93
  258.4 3.2 convolution_bitcast_fusion.3
  261.6 2.7 fusion.91
  265.5 1.9 copy.130
  267.4 2.7 maximum_add_fusion.2
  270.1 1.9 copy.131
  274.5 2.5 fusion.95
  277.0 4.7 fusion.94
  285.4 5.4 fusion.90
  290.8 5.3 fusion.92
  296.1 2.0 fusion.93
  298.1 3.2 convolution_bitcast_fusion.3
  301.3 2.7 fusion.91
  305.3 1.9 copy.130
  307.2 2.7 maximum_add_fusion.2
  309.9 1.9 copy.131
  314.2 2.5 fusion.95
  316.7 4.7 fusion.94
  325.5 5.3 collective-permute-done.1
  332.9 1.6 stack.36
  334.6 6.5 %all-to-all-start = ((bf16[8,1024,128]{1,2,0:T(8,128)(2,1)}), bf16[8,1024,128]{1,2,0:T(8,128)(2,1)}, u32[]{:S(2)}, u32[]{:S(2)}) async-start(bf16[8,1024,128]{1,2,0:T(8,128)(2,1)} %stack.36), calls=%async_computation | async-start | bytes 4194304 | tf_op jit(solution)/shard_map/all_to_all | solution.py:132
  341.8 19.7 %all-to-all-done = bf16[8,1024,128]{1,2,0:T(8,128)(2,1)} async-done(((bf16[8,1024,128]{1,2,0:T(8,128)(2,1)}), bf16[8,1024,128]{1,2,0:T(8,128)(2,1)}, u32[]{:S(2)}, u32[]{:S(2)}) %all-to-all-start) | async-done | bytes 2097184 | tf_op jit(solution)/shard_map/all_to_all | solution.py:132
  361.5 3.2 fusion.46
  366.3 52.2 %all-gather.9.cloned.1.call-done = bf16[1,1024,1,1024]{3,1,2,0:T(8,128)(2,1)} async-done(((bf16[1,1024,1,128]{3,1,2,0:T(8,128)(2,1)}), bf16[1,1024,1,1024]{3,1,2,0:T(8,128)(2,1)}) %all-gather.9.cloned.1.call-update) | async-done | bytes 2097168 | tf_op jit(solution)/shard_map/all_gather | solution.py:134
  418.6 4.3 fusion.47
  422.8 2.6 copy.110
  426.8 1.8 copy.88
  428.6 1.6 copy.90
  434.2 3.9 fusion.41
  438.1 4.4 add_convert_fusion
  442.5 70.5 %reduce-scatter.17.cloned.1.call-done = bf16[32,672]{1,0:T(8,128)(2,1)} async-done(((bf16[1024,672]{1,0:T(8,128)(2,1)}), bf16[32,672]{1,0:T(8,128)(2,1)}) %reduce-scatter.17.cloned.1.call-update) | async-done | bytes 43024
  514.8 89.8 %reduce-scatter.19.cloned.1.call-done = bf16[32,672]{1,0:T(8,128)(2,1)} async-done(((bf16[1024,672]{1,0:T(8,128)(2,1)}), bf16[32,672]{1,0:T(8,128)(2,1)}) %reduce-scatter.19.cloned.1.call-update) | async-done | bytes 43024
  (165 shorter events, 37.1 us)
Async XLA Ops:
  7.2 59.4 %copy-start = (bf16[1024,672]{0,1:T(8,128)(2,1)S(1)}, bf16[1024,672]{0,1:T(8,128)(2,1)}, u32[]{:S(2)}) copy-start(bf16[1024,672]{0,1:T(8,128)(2,1)} %param.14) | copy-start | bytes 4128772
  7.2 59.4 %all-gather.5.cloned.1.call-start = ((), (), s32[]{:S(2)}) async-start(), calls=%async_computation.5 | async-start | bytes 1622016 | tf_op jit(solution)/shard_map/all_gather | solution.py:55
  7.9 111.6 %all-gather.7.cloned.1.call-start = ((), (), s32[]{:S(2)}) async-start(), calls=%async_computation.6 | async-start | bytes 1622016 | tf_op jit(solution)/shard_map/all_gather | solution.py:56
  8.7 163.9 %reduce-scatter.13.cloned.1.call-start = ((), (), s32[]{:S(2)}) async-start(), calls=%async_computation.8 | async-start | bytes 2359296
  72.5 156.9 %reduce-scatter.15.cloned.1.call-start = ((), (), s32[]{:S(2)}) async-start(), calls=%async_computation.9 | async-start | bytes 2359296
  126.6 112.0 %copy-start.9 = (bf16[1024,256]{0,1:T(8,128)(2,1)}, bf16[1024,256]{0,1:T(8,128)(2,1)S(1)}, u32[]{:S(2)}) copy-start(bf16[1024,256]{0,1:T(8,128)(2,1)S(1)} %copy.80) | copy-start | bytes 1572868
  126.6 104.6 %copy-start.27 = (f32[128]{0:T(128)S(1)}, f32[128]{0:T(128)}, u32[]{:S(2)}) copy-start(f32[128]{0:T(128)} %param.19) | copy-start | bytes 1540
  126.7 111.8 %copy-start.7 = (f32[1024,256]{0,1:T(8,128)}, f32[1024,256]{0,1:T(8,128)S(1)}, u32[]{:S(2)}) copy-start(f32[1024,256]{0,1:T(8,128)S(1)} %convert_element_type.99) | copy-start | bytes 3145732
  126.8 111.7 %copy-start.21 = (f32[1024,2]{0,1:T(2,128)}, f32[1024,2]{0,1:T(2,128)S(1)}, u32[]{:S(2)}) copy-start(f32[1024,2]{0,1:T(2,128)S(1)} %multiply_reduce_fusion.1) | copy-start | bytes 24580
  126.8 111.7 %copy-start.29 = (f32[128]{0:T(128)S(1)}, f32[128]{0:T(128)}, u32[]{:S(2)}) copy-start(f32[128]{0:T(128)} %param.18) | copy-start | bytes 1540
  173.7 65.8 %copy-start.11 = (bf16[1024,128]{1,0:T(8,128)(2,1)}, bf16[1024,128]{1,0:T(8,128)(2,1)S(1)}, u32[]{:S(2)}) copy-start(bf16[1024,128]{1,0:T(8,128)(2,1)S(1)} %copy.105) | copy-start | bytes 786436
  174.0 59.2 %copy-start.25 = (f32[1024]{0:T(1024)}, f32[1024]{0:T(1024)S(1)}, u32[]{:S(2)}) copy-start(f32[1024]{0:T(1024)S(1)} %fusion.52) | copy-start | bytes 12292
  174.0 59.2 %copy-start.23 = (f32[1024]{0:T(1024)}, f32[1024]{0:T(1024)S(1)}, u32[]{:S(2)}) copy-start(f32[1024]{0:T(1024)S(1)} %fusion.59) | copy-start | bytes 12292
  233.2 6.4 %collective-permute-start = (bf16[2,1024,1,128]{3,1,2,0:T(8,128)(2,1)}, bf16[2,1024,1,128]{3,1,2,0:T(8,128)(2,1)}, u32[]{:S(2)}, u32[]{:S(2)}) collective-permute-start(bf16[2,1024,1,128]{3,1,2,0:T(8,128)(2,1)} %pad_maximum_fusion), channel_id=1, source_target_pairs={{0,8},{8,16},{16,24},{24,32},{32,40},{40,48},{48,56},{56,64},{64,7... | collective-permute-start | bytes 1572872 | tf_op jit(solution)/shard_map/ppermute | solution.py:15
  239.6 3.6 dynamic-slice-start
  245.6 5.4 copy-start.3
  251.0 5.3 slice-start
  251.1 5.3 slice-start.1
  251.1 5.3 copy-start.4
  258.4 3.2 copy-start.1
  258.4 3.2 copy-start.15
  261.6 2.7 copy-start.6
  272.0 2.5 copy-start.2
  274.5 2.5 copy-start.5
  277.0 4.9 copy-start.16
  285.4 5.4 copy-start.3
  290.8 5.3 slice-start
  290.8 5.3 slice-start.1
  290.8 5.3 copy-start.4
  298.1 3.3 copy-start.1
  298.1 3.2 copy-start.15
  301.3 2.7 copy-start.6
  311.8 2.5 copy-start.2
  314.2 2.5 copy-start.5
  316.7 4.9 copy-start.16
  322.6 9.5 %copy-start.12 = (bf16[1024,128]{1,0:T(8,128)(2,1)S(1)}, bf16[1024,128]{1,0:T(8,128)(2,1)}, u32[]{:S(2)}) copy-start(bf16[1024,128]{1,0:T(8,128)(2,1)} %copy-done.11) | copy-start | bytes 786436
  322.6 9.5 %copy-start.28 = (f32[128]{0:T(128)S(1)}, f32[128]{0:T(128)}, u32[]{:S(2)}) copy-start(f32[128]{0:T(128)} %param.19) | copy-start | bytes 1540
  322.6 9.7 %copy-start.26 = (f32[1024]{0:T(1024)S(1)}, f32[1024]{0:T(1024)}, u32[]{:S(2)}) copy-start(f32[1024]{0:T(1024)} %copy-done.25) | copy-start | bytes 12292
  322.7 9.8 %copy-start.24 = (f32[1024]{0:T(1024)S(1)}, f32[1024]{0:T(1024)}, u32[]{:S(2)}) copy-start(f32[1024]{0:T(1024)} %copy-done.23) | copy-start | bytes 12292
  324.0 6.8 %collective-permute-start.1 = (bf16[2,1024,1,128]{3,1,2,0:T(8,128)(2,1)S(1)}, bf16[2,1024,1,128]{3,1,2,0:T(8,128)(2,1)S(1)}, u32[]{:S(2)}, u32[]{:S(2)}) collective-permute-start(bf16[2,1024,1,128]{3,1,2,0:T(8,128)(2,1)S(1)} %slice.69), channel_id=1, source_target_pairs={{8,0},{16,8},{24,16},{32,24},{40,32},{48,40},{56,48},{64,56},{72,6... | collective-permute-start | bytes 1572872 | tf_op jit(solution)/shard_map/ppermute | solution.py:15
  334.6 26.9 %all-to-all-start = ((bf16[8,1024,128]{1,2,0:T(8,128)(2,1)}), bf16[8,1024,128]{1,2,0:T(8,128)(2,1)}, u32[]{:S(2)}, u32[]{:S(2)}) async-start(bf16[8,1024,128]{1,2,0:T(8,128)(2,1)} %stack.36), calls=%async_computation | async-start | bytes 4194304 | tf_op jit(solution)/shard_map/all_to_all | solution.py:132
  341.0 77.5 %all-gather.9.cloned.1.call-start = ((), (), s32[]{:S(2)}) async-start(), calls=%async_computation.7 | async-start | bytes 2359296 | tf_op jit(solution)/shard_map/all_gather | solution.py:134
  341.8 171.2 %reduce-scatter.17.cloned.1.call-start = ((), (), s32[]{:S(2)}) async-start(), calls=%async_computation.10 | async-start | bytes 1622016
  366.3 238.3 %reduce-scatter.19.cloned.1.call-start = ((), (), s32[]{:S(2)}) async-start(), calls=%async_computation.11 | async-start | bytes 1622016
  422.8 2.7 copy-start.30
  422.8 2.7 copy-start.13
  428.6 3.2 copy-start.8
  434.2 3.9 copy-start.31
  (8 other events, 10.2 us)
Sparse Core Ops, SparseCore 0:
  10.6 55.9 all-gather.4
  69.1 50.2 all-gather.6
  122.0 50.5 reduce-scatter.12
  175.0 54.3 reduce-scatter.14
  343.8 74.6 all-gather.8
  422.2 90.7 reduce-scatter.16
  516.9 87.6 reduce-scatter.18
